TPU v7x, 256 devices: a whole 4x4x8 slice. The times are simulated.
256 devices in a mesh: dp: 32 (over z, x_hi, core), tensor: 8 (over x_lo, y).
Axes of the slice: x: 4 (x_hi: 2, x_lo: 2; x = x_hi * 2 + x_lo), y: 4, z: 8, core: 2. Of those that a mesh axis runs over, the one named last changes fastest.
Arguments:
- hidden: bfloat16 [16384, 14336], P('dp', 'tensor'), may hold values from -76 to 76
- base_weight: bfloat16 [14336, 4096], P('tensor', 'dp'), may hold values from -0.046875 to 0.046875
- adapter_in: bfloat16 [256, 14336], P(None, 'tensor'), may hold values from -0.046875 to 0.046875
- adapter_out: bfloat16 [256, 4096], P(None, 'tensor'), may hold values from -0.375 to 0.375
- cotangent: bfloat16 [16384, 4096], P('dp', 'tensor'), may hold values from -0.046875 to 0.046875
Outputs:
- output: bfloat16 [16384, 4096], P('dp', 'tensor')
- grad_in: float32 [256, 14336], P('dp', 'tensor')
- grad_out: float32 [256, 4096], P('dp', 'tensor')
All inputs are finite; a program needn't handle non-finite values.
Results may differ from a plain program's by a relative error of at most 0.0031.
Values may be sent and summed in bfloat16 or wider, within the bound.
A program may use at most 128 MiB of HBM per device.

v0:
```python
import jax
import jax.numpy as jnp
from jax import lax
from jax.sharding import PartitionSpec as P

adapter_scale = 4.0
exp_rate = 0.25
tiny_eps = 1e-06


def inverse_sinh(value):
    return jnp.log(value + jnp.sqrt(1.0 + value * value))


def shards(hidden, base_weight, adapter_in, adapter_out, cotangent):
    feature_count = hidden.shape[1] * lax.axis_size("tensor")
    contract_last = (((1,), (1,)), ((), ()))
    contract_first = (((0,), (0,)), ((), ()))
    square_part = jnp.sum(jnp.square(hidden.astype(jnp.float32)), axis=1)
    rank_part = lax.dot_general(
        hidden, adapter_in, contract_last, preferred_element_type=jnp.float32
    )
    square_sum, lorentz_raw = lax.psum((square_part, rank_part), "tensor")
    level = jnp.sqrt(square_sum / feature_count + tiny_eps)
    radius = exp_rate * level
    lift_factor = jnp.sinh(radius) / radius
    lorentz = lift_factor[:, None] * lorentz_raw
    norm_value = jnp.sqrt(jnp.sum(lorentz * lorentz, axis=1) + tiny_eps)
    phi_value = inverse_sinh(norm_value) / norm_value
    tangent = (phi_value[:, None] * lorentz).astype(jnp.bfloat16)
    partial_cols = jnp.dot(
        hidden,
        lax.all_gather(base_weight, "dp", axis=1, tiled=True),
        preferred_element_type=jnp.float32,
    )
    base_sum = lax.psum_scatter(partial_cols, "tensor", scatter_dimension=1, tiled=True)
    adapter_term = jnp.dot(tangent, adapter_out, preferred_element_type=jnp.float32)
    output = (base_sum + adapter_scale * adapter_term).astype(jnp.bfloat16)
    out_part = adapter_scale * lax.dot_general(
        tangent, cotangent, contract_first, preferred_element_type=jnp.float32
    )
    cotan_later = adapter_scale * lax.dot_general(
        cotangent, adapter_out, contract_last, preferred_element_type=jnp.float32
    )
    tangent_grad = lax.psum(cotan_later, "tensor")
    inner_value = jnp.sum(lorentz * tangent_grad, axis=1)
    coefficient = (1.0 / jnp.sqrt(1.0 + norm_value * norm_value) - phi_value) / (
        norm_value * norm_value
    )
    lorentz_grad = (
        phi_value[:, None] * tangent_grad + (coefficient * inner_value)[:, None] * lorentz
    )
    raw_grad = (lift_factor[:, None] * lorentz_grad).astype(jnp.bfloat16)
    in_part = lax.dot_general(raw_grad, hidden, contract_first, preferred_element_type=jnp.float32)
    grad_in, grad_out = (
        lax.psum_scatter(in_part, "dp", scatter_dimension=0, tiled=True),
        lax.psum_scatter(out_part, "dp", scatter_dimension=0, tiled=True),
    )
    return (output, grad_in, grad_out)


def solution(mesh):
    return jax.shard_map(
        shards,
        mesh=mesh,
        in_specs=(
            P("dp", "tensor"),
            P("tensor", "dp"),
            P(None, "tensor"),
            P(None, "tensor"),
            P("dp", "tensor"),
        ),
        out_specs=(P("dp", "tensor"), P("dp", "tensor"), P("dp", "tensor")),
        check_vma=False,
    )
```

profile of v0, /device:TPU:6, one launch (start us, length us, event | category | flops | bytes accessed | tf_op | source)
XLA Modules:
  0.0 505.3 jit_solution(1643194782338314883)
XLA Ops:
  8.0 0.0 all-gather.2.cloned.1.call-start
  8.1 0.7 all-gather.2.cloned.1.call-update
  8.7 0.0 all-reduce.3.cloned.1.call-start
  8.8 2.2 convolution_multiply_fusion.2
  11.0 3.1 fusion.12
  14.1 0.0 all-reduce.3.cloned.1.call-update
  14.2 0.0 reduce-scatter.4.cloned.1.call-start
  14.2 139.5 %all-gather.2.cloned.1.call-done = bf16[1792,4096]{1,0:T(8,128)(2,1)} async-done(((bf16[1792,128]{1,0:T(8,128)(2,1)}), bf16[1792,4096]{1,0:T(8,128)(2,1)}) %all-gather.2.cloned.1.call-update) | async-done | bytes 14680080 | tf_op jit(solution)/shard_map/all_gather | solution.py:33
  153.7 13.0 %fusion.11 = f32[512,4096]{1,0:T(8,128)} fusion(bf16[512,1792]{1,0:T(8,128)(2,1)S(1)} %copy-done.2, bf16[1792,4096]{1,0:T(8,128)(2,1)} %all-gather.2.cloned.1.call-done), kind=kOutput, calls=%fused_computation.25 | convolution fusion | flops 7516192768 | bytes 24903680 | tf_op jit(solution)/shard_map/dot_general | solution.py:31
  166.7 0.0 reduce-scatter.4.cloned.1.call-update
  166.7 0.0 reduce-scatter.8.cloned.1.call-start
  166.8 0.4 multiply_reduce_fusion
  167.2 18.2 %psum.21 = f32[512]{0:T(512)S(1)} all-reduce(f32[512]{0:T(512)S(1)} %multiply_reduce_fusion), channel_id=1, replica_groups=mesh['dp'=32,'tensor'=8] {'tensor'}, use_global_device_ids=true, to_apply=%region_2.0 | all-reduce | flops 512 | bytes 4096 | tf_op jit(solution)/shard_map/psum | solution.py:23
  185.4 0.0 all-reduce.3.cloned.1.call-done
  185.4 1.6 multiply_reduce_fusion.1
  187.0 2.6 convolution_multiply_fusion.1
  189.7 0.0 reduce-scatter.8.cloned.1.call-update
  189.7 0.0 reduce-scatter.6.cloned.1.call-start
  189.7 3.2 fusion.2
  192.9 0.0 reduce-scatter.6.cloned.1.call-update
  192.9 66.8 %reduce-scatter.4.cloned.1.call-done = f32[512,512]{1,0:T(8,128)} async-done(((f32[512,4096]{1,0:T(8,128)}), f32[512,512]{1,0:T(8,128)}) %reduce-scatter.4.cloned.1.call-update) | async-done | bytes 1048592 | tf_op jit(solution)/shard_map/reduce_scatter | solution.py:36
  259.7 2.4 fusion.1
  262.1 114.0 %reduce-scatter.8.cloned.1.call-done = f32[8,512]{1,0:T(8,128)} async-done(((f32[256,512]{1,0:T(8,128)}), f32[8,512]{1,0:T(8,128)}) %reduce-scatter.8.cloned.1.call-update) | async-done | bytes 16400 | tf_op jit(solution)/shard_map/reduce_scatter | solution.py:57
  376.1 121.6 %reduce-scatter.6.cloned.1.call-done = f32[8,1792]{1,0:T(8,128)} async-done(((f32[256,1792]{1,0:T(8,128)}), f32[8,1792]{1,0:T(8,128)}) %reduce-scatter.6.cloned.1.call-update) | async-done | bytes 57360 | tf_op jit(solution)/shard_map/reduce_scatter | solution.py:56
  (10 shorter events, 0.1 us)
Async XLA Ops:
  8.0 3.0 copy-start
  8.0 145.7 %all-gather.2.cloned.1.call-start = ((), (), s32[]{:S(2)}) async-start(), calls=%async_computation.3 | async-start | bytes 15138816 | tf_op jit(solution)/shard_map/all_gather | solution.py:33
  8.7 176.7 %all-reduce.3.cloned.1.call-start = ((), (), s32[]{:S(2)}) async-start(), calls=%async_computation.7 | async-start | bytes 2097152 | tf_op jit(solution)/shard_map/psum | solution.py:23
  11.0 142.6 %copy-start.2 = (bf16[512,1792]{1,0:T(8,128)(2,1)S(1)}, bf16[512,1792]{1,0:T(8,128)(2,1)}, u32[]{:S(2)}) copy-start(bf16[512,1792]{1,0:T(8,128)(2,1)} %param.5) | copy-start | bytes 5505028
  14.2 245.6 %reduce-scatter.4.cloned.1.call-start = ((), (), s32[]{:S(2)}) async-start(), calls=%async_computation.4 | async-start | bytes 9437184 | tf_op jit(solution)/shard_map/reduce_scatter | solution.py:36
  166.7 209.4 %reduce-scatter.8.cloned.1.call-start = ((), (), s32[]{:S(2)}) async-start(), calls=%async_computation.6 | async-start | bytes 540672 | tf_op jit(solution)/shard_map/reduce_scatter | solution.py:57
  185.4 4.3 copy-start.1
  189.7 308.0 %reduce-scatter.6.cloned.1.call-start = ((), (), s32[]{:S(2)}) async-start(), calls=%async_computation.5 | async-start | bytes 1892352 | tf_op jit(solution)/shard_map/reduce_scatter | solution.py:56
  192.9 66.8 %copy-start.3 = (bf16[256,512]{1,0:T(8,128)(2,1)S(1)}, bf16[256,512]{1,0:T(8,128)(2,1)}, u32[]{:S(2)}) copy-start(bf16[256,512]{1,0:T(8,128)(2,1)} %param.8) | copy-start | bytes 786436
Sparse Core Ops, SparseCore 0:
  11.4 142.2 all-gather.1
Sparse Core Ops, SparseCore 1:
  14.2 126.8 all-reduce.2
  166.8 92.9 reduce-scatter.3
  264.2 111.9 reduce-scatter.7
  381.4 116.3 reduce-scatter.5
where the time goes:
time: 507 us; the launch traced here: 505 us
  waiting for transfers between devices  443 us (87%)
  matrix products  26.5 us (5%)
  blocking collectives  18.2 us (4%)
  between operations  15.7 us (3%)
    all_gather x1, waiting for transfers between devices, shards(): lax.all_gather(base_weight, 'dp', axis=1, tiled=True)  139 us
    reduce_scatter x1, waiting for transfers between devices, shards(): lax.psum_scatter(in_part, 'dp', scatter_dimension=0, tiled=True)  122 us
    reduce_scatter x1, waiting for transfers between devices, shards(): lax.psum_scatter(out_part, 'dp', scatter_dimension=0, tiled=True)  114 us
    reduce_scatter x1, waiting for transfers between devices, shards(): lax.psum_scatter(partial_cols, 'tensor', scatter_dimension=1, tiled=True)  66.8 us
    psum x1, blocking collectives, shards(): square_sum, lorentz_raw = lax.psum((square_part, rank_part), 'tensor')  18.2 us
    dot_general x1, matrix products, shards(): jnp.dot(hidden, lax.all_gather(base_weight, 'dp', axis=1, tiled=True), pr...  13 us
  transfers between devices with their start and end apart: 5, of which 4 were waited for; matrix products, arithmetic and copies ran while one was open for 6% of the time, Pallas kernels for 0%

commit v1 on v0

v1 whole, which is shorter than its diff:
```python
import functools

import jax
import jax.numpy as jnp
from jax import lax
from jax.experimental import pallas as pl
from jax.experimental.pallas import tpu as pltpu
from jax.sharding import PartitionSpec as P

adapter_scale = 4.0
exp_rate = 0.25
tiny_eps = 1e-06

MESH = pl.DeviceIdType.MESH
NZ, NY, NT = 8, 4, 8
F32, BF16 = jnp.float32, jnp.bfloat16
LAST = (((1,), (1,)), ((), ()))
FIRST = (((0,), (0,)), ((), ()))
LAG = 4


def lift_of(radius):
    sq = radius * radius
    series = 1.0 + sq / 6.0 * (
        1.0 + sq / 20.0 * (1.0 + sq / 42.0 * (1.0 + sq / 72.0 * (1.0 + sq / 110.0)))
    )
    direct = (jnp.exp(radius) - jnp.exp(-radius)) / (2.0 * radius)
    return jnp.where(radius < 1.0, series, direct)


def kernel(
    features,
    hid_hbm, b_hbm, ain_hbm, aout_hbm, cot_hbm,
    out_ref, gin_ref, gout_ref,
    hid, ain, aout, cot, weights, psend, precv, acc, xsend, xrecv,
    rsend, rrecv, td, gpart, g1recv, g2send, g2recv, g3send, g3recv, adapt,
    local_sem, bsend, bsend2, brecv, ssend, srecv, csend_sem, crecv_sem,
    xsend_sem, xrecv_sem, rsend_sem, rrecv_sem, asend_sem, arecv_sem,
    g12send_sem, g12recv_sem, g3send_sem, g3recv_sem,
):
    d, t = lax.axis_index("dp"), lax.axis_index("tensor")
    z, h, c = d // 4, (d // 2) % 2, d % 2
    xl, y = t // NY, t % NY
    tokens = hid.shape[0]

    def at(z_, h_, c_):
        return (z_ * 4 + h_ * 2 + c_, t)

    zup, zdown = at((z + 1) % NZ, h, c), at((z + NZ - 1) % NZ, h, c)
    partner, sibling = at(z, 1 - h, c), at(z, h, 1 - c)

    loads = [
        pltpu.make_async_copy(b_hbm, weights.at[z, h, c], local_sem.at[0]),
        pltpu.make_async_copy(hid_hbm, hid, local_sem.at[1]),
        pltpu.make_async_copy(ain_hbm, ain, local_sem.at[2]),
        pltpu.make_async_copy(cot_hbm, cot, local_sem.at[3]),
        pltpu.make_async_copy(aout_hbm, aout, local_sem.at[4]),
    ]
    for load in loads:
        load.start()

    barrier = pltpu.get_barrier_semaphore()
    peers = [at((z + i) % NZ, h, c) for i in range(1, NZ)]
    peers += [(d, (t + j) % NT) for j in range(1, NT)]
    peers += [partner, sibling]
    for peer in peers:
        pl.semaphore_signal(barrier, inc=1, device_id=peer, device_id_type=MESH)
    pl.semaphore_wait(barrier, len(peers))

    def remote(src, dst, send, recv, peer):
        return pltpu.make_async_remote_copy(
            src_ref=src, dst_ref=dst, send_sem=send, recv_sem=recv,
            device_id=peer, device_id_type=MESH,
        )

    def place(p):
        slot, way = p // 2, p % 2
        hops = (slot + 1) // 2
        flag = jnp.where((slot == 0) | (slot == 7), way, (slot + 1) % 2)
        zs = (z + NZ + (2 * way - 1) * hops) % NZ
        return zs, (h + flag) % 2

    def z_copy(p, q, peer, send):
        zs, hs = place(p)
        ref = weights.at[zs, hs, c]
        return remote(ref, ref, send, brecv.at[q], peer)

    def sib_copy(p):
        zs, hs = place(p)
        ref = weights.at[zs, hs, c]
        return remote(ref, ref, ssend.at[p], srecv.at[p], sibling)

    def seed_copy():
        ref = weights.at[z, h, c]
        return remote(ref, ref, bsend2.at[2], brecv.at[1], partner)

    loads[0].wait()
    z_copy(0, 2, zup, bsend.at[0]).start()
    z_copy(0, 3, zdown, bsend2.at[0]).start()
    seed_copy().start()

    blk = tokens // NT
    eye = lax.broadcasted_iota(jnp.int32, (blk, blk), 0) == lax.broadcasted_iota(
        jnp.int32, (blk, blk), 1
    )
    for load in loads[1:]:
        load.wait()

    def rank_part(m, carry):
        rows = pl.ds(pl.multiple_of(m * 256, 256), 256)
        left = hid[rows, :]
        raw = lax.dot_general(left, ain[...], LAST, preferred_element_type=F32)
        wide = left.astype(F32)
        square = jnp.sum(wide * wide, axis=1, keepdims=True)
        later = lax.dot_general(cot[rows, :], aout[...], LAST, preferred_element_type=F32)
        for jj in range(256 // blk):
            j = m * (256 // blk) + jj
            cut = slice(jj * blk, (jj + 1) * blk)
            rsend[j, 0:blk, 0:256] = raw[cut]
            rsend[j, 0:blk, 256:512] = later[cut]
            rsend[j, blk : blk + 8, :] = jnp.zeros((8, 512), F32)
            rsend[j, blk : blk + 1, 0:blk] = jnp.sum(
                jnp.where(eye, square[cut], 0.0), axis=0, keepdims=True
            )
        return carry

    lax.fori_loop(0, tokens // 256, rank_part, 0)

    def rank_copy(j):
        to = (t + j) % NT
        return remote(
            rsend.at[to], rrecv.at[j - 1], rsend_sem.at[j - 1], rrecv_sem.at[j - 1], (d, to)
        )

    def td_copy(j):
        to = (t + j) % NT
        return remote(td.at[t], td.at[t], asend_sem.at[j - 1], arecv_sem.at[j - 1], (d, to))

    def td_arrival(j):
        ref = td.at[(t + NT - j) % NT]
        return remote(ref, ref, asend_sem.at[j - 1], arecv_sem.at[j - 1], (d, (t + j) % NT))

    for j in range(1, NT):
        rank_copy(j).start()

    def tangent_step():
        for j in range(1, NT):
            rank_copy(j).wait_recv()
        total = rsend[t]
        for j in range(1, NT):
            total = total + rrecv[j - 1]
        square_sum = jnp.sum(
            jnp.where(eye, total[blk : blk + 1, 0:blk], 0.0), axis=1, keepdims=True
        )
        lorentz_raw, later = total[:blk, 0:256], adapter_scale * total[:blk, 256:512]
        level = jnp.sqrt(square_sum / features + tiny_eps)
        lift = lift_of(exp_rate * level)
        lorentz = lift * lorentz_raw
        norm = jnp.sqrt(jnp.sum(lorentz * lorentz, axis=1, keepdims=True) + tiny_eps)
        root = jnp.sqrt(1.0 + norm * norm)
        phi = jnp.log(norm + root) / norm
        inner = jnp.sum(lorentz * later, axis=1, keepdims=True)
        coefficient = (1.0 / root - phi) / (norm * norm)
        dlorentz = phi * later + (coefficient * inner) * lorentz
        td[t, 0] = (phi * lorentz).astype(BF16)
        td[t, 1] = (lift * dlorentz).astype(BF16)
        for j in range(1, NT):
            td_copy(j).start()

    width = gpart.shape[-1]
    half = width // 2

    def g1_copy():
        return remote(gpart.at[1 - c], g1recv, g12send_sem.at[0], g12recv_sem.at[0], sibling)

    def g2_copy():
        return remote(g2send, g2recv, g12send_sem.at[1], g12recv_sem.at[1], partner)

    def g3_copy(i):
        to = (z + i) % NZ
        return remote(
            g3send.at[to], g3recv.at[i - 1], g3send_sem.at[i - 1], g3recv_sem.at[i - 1],
            at(to, h, c),
        )

    def grad_step():
        for j in range(1, NT):
            td_arrival(j).wait_recv()
        tangent = td[:, 0].reshape(tokens, 256)
        draw = td[:, 1].reshape(tokens, 256)

        def put(value, cols):
            for k in range(32):
                gpart[k % 2, (k // 2) % 2, k // 4, :, cols] = value[k * 8 : (k + 1) * 8]

        def in_tile(n, carry):
            cols = pl.ds(pl.multiple_of(n * 256, 256), 256)
            put(lax.dot_general(draw, hid[:, cols], FIRST, preferred_element_type=F32), cols)
            return carry

        lax.fori_loop(0, hid.shape[1] // 256, in_tile, 0)
        for n in range(2):
            cols = slice(n * 256, (n + 1) * 256)
            part = lax.dot_general(tangent, cot[:, cols], FIRST, preferred_element_type=F32)
            put(adapter_scale * part, slice(hid.shape[1] + n * 256, hid.shape[1] + (n + 1) * 256))
        g1_copy().start()
        for n in range(2):
            adapt[n] = adapter_scale * jnp.dot(
                tangent, aout[:, n * 256 : (n + 1) * 256], preferred_element_type=F32
            )

    def grad_two():
        g1_copy().wait_recv()
        g2send[...] = (gpart[c, 1 - h] + g1recv[1 - h]).reshape(64, width).astype(BF16)
        g2_copy().start()
        gpart[c, h] = gpart[c, h] + g1recv[h]

    def grad_three():
        g2_copy().wait_recv()
        gpart[c, h] = gpart[c, h] + g2recv[...].astype(F32).reshape(NZ, 8, width)
        for k in range(NZ):
            block = gpart[c, h, k]
            g3send[k] = jnp.concatenate([block[:, :half], block[:, half:]], axis=0).astype(BF16)
        for i in range(1, NZ):
            g3_copy(i).start()

    def grad_last():
        block = gpart[c, h, z]
        total = jnp.concatenate([block[:, :half], block[:, half:]], axis=0)
        for i in range(1, NZ):
            g3_copy(i).wait_recv()
            total = total + g3recv[i - 1].astype(F32)
        cut = hid.shape[1] - half
        gin_ref[:, :half] = total[:8]
        gin_ref[:, half:] = total[8:, :cut]
        gout_ref[...] = total[8:, cut:]

    def part_copy(p):
        zs, hs = place(p)
        to = zs % NY
        idx, src = (zs // NY) * 2 + hs, (y - to + NY - 1) % NY
        return remote(
            psend.at[p], precv.at[idx, src], csend_sem.at[p], crecv_sem.at[idx, src],
            (d, xl * NY + to),
        )

    def part_arrival(idx, src):
        ref = precv.at[idx, src]
        return remote(ref, ref, csend_sem.at[0], crecv_sem.at[idx, src], sibling)

    def x_copy(hs):
        return remote(
            xsend.at[hs], xrecv.at[hs], xsend_sem.at[hs], xrecv_sem.at[hs], (d, (1 - xl) * NY + y)
        )

    def reduce_strip(p):
        zs, hs = place(p)
        idx = (zs // NY) * 2 + hs

        @pl.when(zs % NY == y)
        def _():
            for src in range(NY - 1):
                part_arrival(idx, src).wait_recv()
            keep = zs // NY == xl

            def tile(m, carry):
                rows = pl.ds(pl.multiple_of(m * 128, 128), 128)
                value = acc[idx, rows, :]
                for src in range(NY - 1):
                    value = value + precv[idx, src, rows, :].astype(F32)
                acc[idx, rows, :] = value
                xsend[jnp.where(keep, 2, hs), rows, :] = value.astype(BF16)
                return carry

            lax.fori_loop(0, tokens // 128, tile, 0)

            @pl.when(jnp.logical_not(keep))
            def _():
                x_copy(hs).start()

    def step(p, carry):
        zs, hs = place(p)
        way = p % 2

        @pl.when(p >= 1)
        def _():
            z_copy(p, p, sibling, bsend.at[p]).wait_recv()

        @pl.when(p == 1)
        def _():
            z_copy(p, 4, zup, bsend.at[p]).start()
            z_copy(p, 5, zdown, bsend2.at[1]).start()

        @pl.when((p >= 2) & (p <= 10))
        def _():
            z_copy(p, p + 4, at((z + NZ + 1 - 2 * way) % NZ, h, c), bsend.at[p]).start()

        @pl.when(p == 13)
        def _():
            z_copy(p, 15, zdown, bsend.at[p]).start()

        sib_copy(p).start()
        sib_copy_in(p).wait_recv()
        to = zs % NY
        slot = jnp.where(to == y, (zs // NY) * 2 + hs, 4)

        def tile(m, inner):
            rows = pl.ds(pl.multiple_of(m * 256, 256), 256)
            right = jnp.concatenate([weights[zs, hs, 0], weights[zs, hs, 1]], axis=1)
            value = jnp.dot(hid[rows, :], right, preferred_element_type=F32)
            acc[slot, rows, :] = value
            psend[p, rows, :] = value.astype(BF16)
            return inner

        lax.fori_loop(0, tokens // 256, tile, 0)

        @pl.when(to != y)
        def _():
            part_copy(p).start()

        @pl.when(p >= LAG)
        def _():
            reduce_strip(p - LAG)

        @pl.when(p == 3)
        def _():
            tangent_step()

        @pl.when(p == 5)
        def _():
            grad_step()

        @pl.when(p == 7)
        def _():
            grad_two()

        @pl.when(p == 9)
        def _():
            grad_three()

        return carry

    def sib_copy_in(p):
        zs, hs = place(p)
        ref = weights.at[zs, hs, 1 - c]
        return remote(ref, ref, ssend.at[p], srecv.at[p], sibling)

    lax.fori_loop(0, 16, step, 0)

    def late(p, carry):
        reduce_strip(p)
        return carry

    lax.fori_loop(16 - LAG, 16, late, 0)
    grad_last()
    for n in range(2):
        x_copy(n).wait_recv()

        def last(m, carry, n=n):
            rows = pl.ds(pl.multiple_of(m * 128, 128), 128)
            value = acc[xl * 2 + n, rows, :] + xrecv[n, rows, :].astype(F32) + adapt[n, rows, :]
            out_ref[rows, n * 256 : (n + 1) * 256] = value.astype(BF16)
            return carry

        lax.fori_loop(0, tokens // 128, last, 0)

    z_copy(0, 2, zup, bsend.at[0]).wait_send()
    z_copy(0, 3, zdown, bsend2.at[0]).wait_send()
    seed_copy().wait_send()
    z_copy(1, 5, zdown, bsend2.at[1]).wait_send()

    def drain(p, carry):
        @pl.when(((p >= 1) & (p <= 10)) | (p == 13))
        def _():
            z_copy(p, p, zup, bsend.at[p]).wait_send()

        sib_copy(p).wait_send()
        zs, hs = place(p)

        @pl.when(zs % NY != y)
        def _():
            part_copy(p).wait_send()

        return carry

    lax.fori_loop(0, 16, drain, 0)
    for n in range(2):
        x_copy(n).wait_send()
    for j in range(1, NT):
        rank_copy(j).wait_send()
        td_copy(j).wait_send()
        g3_copy(j).wait_send()
    g1_copy().wait_send()
    g2_copy().wait_send()


def shards(hidden, base_weight, adapter_in, adapter_out, cotangent):
    tokens, ff = hidden.shape
    rank, cols = adapter_out.shape
    features = ff * lax.axis_size("tensor")
    width = ff + cols
    dma = pltpu.SemaphoreType.DMA
    hbm = pl.BlockSpec(memory_space=pl.ANY)
    vmem = pl.BlockSpec(memory_space=pltpu.VMEM)
    output, grad_in, grad_out = pl.pallas_call(
        functools.partial(kernel, features),
        out_shape=(
            jax.ShapeDtypeStruct((tokens, cols), BF16),
            jax.ShapeDtypeStruct((8, ff), F32),
            jax.ShapeDtypeStruct((8, cols), F32),
        ),
        in_specs=[hbm] * 5,
        out_specs=(vmem,) * 3,
        scratch_shapes=[
            pltpu.VMEM((tokens, ff), BF16),
            pltpu.VMEM((rank, ff), BF16),
            pltpu.VMEM((rank, cols), BF16),
            pltpu.VMEM((tokens, cols), BF16),
            pltpu.VMEM((NZ, 2, 2, ff, 128), BF16),
            pltpu.VMEM((16, tokens, 256), BF16),
            pltpu.VMEM((4, 3, tokens, 256), BF16),
            pltpu.VMEM((5, tokens, 256), F32),
            pltpu.VMEM((3, tokens, 256), BF16),
            pltpu.VMEM((2, tokens, 256), BF16),
            pltpu.VMEM((NT, tokens // NT + 8, 512), F32),
            pltpu.VMEM((NT - 1, tokens // NT + 8, 512), F32),
            pltpu.VMEM((NT, 2, tokens // NT, rank), BF16),
            pltpu.VMEM((2, 2, NZ, 8, width), F32),
            pltpu.VMEM((2, NZ, 8, width), F32),
            pltpu.VMEM((NZ * 8, width), BF16),
            pltpu.VMEM((NZ * 8, width), BF16),
            pltpu.VMEM((NZ, 16, width // 2), BF16),
            pltpu.VMEM((NZ - 1, 16, width // 2), BF16),
            pltpu.VMEM((2, tokens, 256), F32),
            dma((5,)),
            dma((16,)),
            dma((3,)),
            dma((16,)),
            dma((16,)),
            dma((16,)),
            dma((16,)),
            dma((4, 3)),
            dma((2,)),
            dma((2,)),
            dma((7,)),
            dma((7,)),
            dma((7,)),
            dma((7,)),
            dma((2,)),
            dma((2,)),
            dma((7,)),
            dma((7,)),
        ],
        compiler_params=pltpu.CompilerParams(
            collective_id=0, has_side_effects=True, vmem_limit_bytes=56 << 20
        ),
        name="adapter_step",
    )(hidden, base_weight, adapter_in, adapter_out, cotangent)
    return (output, grad_in, grad_out)


def solution(mesh):
    return jax.shard_map(
        shards,
        mesh=mesh,
        in_specs=(
            P("dp", "tensor"),
            P("tensor", "dp"),
            P(None, "tensor"),
            P(None, "tensor"),
            P("dp", "tensor"),
        ),
        out_specs=(P("dp", "tensor"), P("dp", "tensor"), P("dp", "tensor")),
        check_vma=False,
    )
```

time: 507 us -> 144 us (0.28)
  waiting for transfers between devices: 443 us -> 0 us
  Pallas kernels: 0 us -> 138 us
  matrix products: 26.5 us -> 0 us
  blocking collectives: 18.2 us -> 0 us
  between operations: 15.7 us -> 0.64 us
    reduce_scatter x3 -> x0, waiting for transfers between devices: 302 us -> none  [the longest x1 122 us: shards(): lax.psum_scatter(in_part, 'dp', scatter_dimension=0, tiled=True)]
    all_gather x1 -> x0, waiting for transfers between devices: 139 us -> none  [shards(): lax.all_gather(base_weight, 'dp', axis=1, tiled=True)]
    pallas_call x0 -> x1, Pallas kernels: none -> 138 us  [shards(): pl.pallas_call(functools.partial(kernel, features), out_shape=(jax.ShapeD...]
    dot_general x6 -> x0, matrix products: 26.5 us -> none  [the longest x1 13 us: shards(): jnp.dot(hidden, lax.all_gather(base_weight, 'dp', axis=1, tiled=True), pr...]
    psum x1 -> x0, blocking collectives: 18.2 us -> none  [shards(): square_sum, lorentz_raw = lax.psum((square_part, rank_part), 'tensor')]
  transfers between devices with their start and end apart: 5 -> 0, of which waited for: 4 -> 0; matrix products, arithmetic and copies ran while one was open for 6% -> 0% of each run, Pallas kernels for 0% -> 0%
where the time goes in v1:
time: 144 us; the launch traced here: 143 us
  Pallas kernels  138 us (96%)
  local copies, waits for them, and re-layouts  4.64 us (3%)
    pallas_call x1, Pallas kernels, shards(): pl.pallas_call(functools.partial(kernel, features), out_shape=(jax.ShapeD...  138 us
    unnamed x3, local copies, waits for them, and re-layouts  4.64 us

profile of v1, /device:TPU:6, one launch (start us, length us, event | category | flops | bytes accessed | tf_op | source)
XLA Modules:
  0.0 143.3 jit_solution(3429544604440357417)
XLA Ops:
  0.6 138.0 %adapter_step.1 = (bf16[512,512]{1,0:T(8,128)(2,1)}, f32[8,1792]{1,0:T(8,128)}, f32[8,512]{1,0:T(8,128)}) custom-call(bf16[512,1792]{1,0:T(8,128)(2,1)} %hid_hbm.1, bf16[1792,128]{1,0:T(8,128)(2,1)} %b_hbm.1, bf16[256,1792]{1,0:T(8,128)(2,1)} %ain_hbm.1, bf16[256,512]{1,0:T(8,128)(2,1)} %aout_hbm.1, bf16[512,512]{1,0:T(8,128)(2,1)} %cot_hbm.1), custom_call_target="tpu_custom_call" | custom-call | tf_op jit(solution)/shard_map/adapter_step/pallas_call | solution.py:405
  138.7 1.9 %copy.11 = bf16[512,512]{1,0:T(8,128)(2,1)} copy(bf16[512,512]{1,0:T(8,128)(2,1)} %get-tuple-element.6) | data formatting | bytes 1048576
  140.5 1.4 %copy.12 = f32[8,1792]{1,0:T(8,128)} copy(f32[8,1792]{1,0:T(8,128)} %get-tuple-element.7) | data formatting | bytes 114688
  142.0 1.3 copy.13

commit v2 on v1

--- a/solution.py
+++ b/solution.py
@@ -16,7 +16,11 @@
 F32, BF16 = jnp.float32, jnp.bfloat16
 LAST = (((1,), (1,)), ((), ()))
 FIRST = (((0,), (0,)), ((), ()))
-LAG = 4
+LAG = 8
+OFFSET = (0, 7, 1, 0, 6, 2, 7, 1, 5, 3, 6, 2, 4, 5, 3, 4)
+OTHER = (0, 0, 0, 1, 0, 0, 1, 1, 0, 0, 1, 1, 0, 1, 1, 1)
+SOURCE = (None, 0, 0, 0, 1, 2, 3, 3, 4, 5, 4, 5, None, 10, 11, 12)
+UP, DOWN = (1, 4, 6, 8, 13), (2, 5, 7, 9, 14)
 
 
 def lift_of(radius):
@@ -34,7 +38,7 @@
     out_ref, gin_ref, gout_ref,
     hid, ain, aout, cot, weights, psend, precv, acc, xsend, xrecv,
     rsend, rrecv, td, gpart, g1recv, g2send, g2recv, g3send, g3recv, adapt,
-    local_sem, bsend, bsend2, brecv, ssend, srecv, csend_sem, crecv_sem,
+    local_sem, bsend, brecv, ssend, srecv, csend_sem, crecv_sem,
     xsend_sem, xrecv_sem, rsend_sem, rrecv_sem, asend_sem, arecv_sem,
     g12send_sem, g12recv_sem, g3send_sem, g3recv_sem,
 ):
@@ -73,31 +77,65 @@
             device_id=peer, device_id_type=MESH,
         )
 
+    deep = hid.shape[1] // 48 * 16
+    cuts = (pl.ds(0, deep), pl.ds(deep, hid.shape[1] - deep))
+
+    def look(p, table):
+        if isinstance(p, int):
+            return table[p]
+        return sum(jnp.where(p == i, v, 0) for i, v in enumerate(table) if v)
+
     def place(p):
-        slot, way = p // 2, p % 2
-        hops = (slot + 1) // 2
-        flag = jnp.where((slot == 0) | (slot == 7), way, (slot + 1) % 2)
-        zs = (z + NZ + (2 * way - 1) * hops) % NZ
-        return zs, (h + flag) % 2
-
-    def z_copy(p, q, peer, send):
+        return (z + look(p, OFFSET)) % NZ, (h + look(p, OTHER)) % 2
+
+    def piece(p, core, part):
         zs, hs = place(p)
-        ref = weights.at[zs, hs, c]
-        return remote(ref, ref, send, brecv.at[q], peer)
-
-    def sib_copy(p):
-        zs, hs = place(p)
-        ref = weights.at[zs, hs, c]
-        return remote(ref, ref, ssend.at[p], srecv.at[p], sibling)
-
-    def seed_copy():
-        ref = weights.at[z, h, c]
-        return remote(ref, ref, bsend2.at[2], brecv.at[1], partner)
+        return weights.at[zs, hs, core, cuts[part]]
+
+    def forward(q, part):
+        if q == 12:
+            up = (part + c) % 2 == 0
+            ref = weights.at[(z + jnp.where(up, 5, 3)) % NZ, h, c, cuts[part]]
+            peer = at((z + jnp.where(up, 1, NZ - 1)) % NZ, h, c)
+        else:
+            ref = piece(SOURCE[q], c, part)
+            peer = zup if q in UP else zdown if q in DOWN else partner
+        return remote(ref, ref, bsend.at[q, part], brecv.at[q, part], peer)
+
+    def arrival(q, part):
+        ref = piece(q, c, part)
+        return remote(ref, ref, bsend.at[q, part], brecv.at[q, part], partner)
+
+    def share(p, part, core):
+        ref = piece(p, core, part)
+        return remote(ref, ref, ssend.at[p, part], srecv.at[p, part], sibling)
 
     loads[0].wait()
-    z_copy(0, 2, zup, bsend.at[0]).start()
-    z_copy(0, 3, zdown, bsend2.at[0]).start()
-    seed_copy().start()
+    for part in range(2):
+        for q in (1, 2, 3):
+            forward(q, part).start()
+    for part in range(2):
+        share(0, part, c).start()
+
+    groups = {
+        1: [[(1, (4,)), (2, (5,))]] * 2,
+        3: [[(3, ())]] * 2,
+        4: [[(4, (6, 10)), (5, (7, 11))]] * 2,
+        6: [[(6, (8,)), (7, (9,))]] * 2,
+        8: [[(8, ()), (9, (12,))]] * 2,
+        10: [[(10, ()), (11, ())]] * 2,
+        12: [[(12, (13, 14, 15))]] * 2,
+        13: [[(13, ()), (14, ())]] * 2,
+        15: [[(15, ())]] * 2,
+    }
+
+    def arrive(first):
+        for part in range(2):
+            for q, onward in groups[first][part]:
+                arrival(q, part).wait_recv()
+                for n in onward:
+                    forward(n, part).start()
+                share(q, part, c).start()
 
     blk = tokens // NT
     eye = lax.broadcasted_iota(jnp.int32, (blk, blk), 0) == lax.broadcasted_iota(
@@ -235,22 +273,27 @@
         gin_ref[:, half:] = total[8:, :cut]
         gout_ref[...] = total[8:, cut:]
 
-    def part_copy(p):
+    tall = tokens // 2
+
+    def part_copy(p, m):
         zs, hs = place(p)
         to = zs % NY
         idx, src = (zs // NY) * 2 + hs, (y - to + NY - 1) % NY
+        rows = pl.ds(m * tall, tall)
         return remote(
-            psend.at[p], precv.at[idx, src], csend_sem.at[p], crecv_sem.at[idx, src],
-            (d, xl * NY + to),
+            psend.at[p, rows], precv.at[idx, src, rows],
+            csend_sem.at[p, m], crecv_sem.at[idx, src, m], (d, xl * NY + to),
         )
 
-    def part_arrival(idx, src):
-        ref = precv.at[idx, src]
-        return remote(ref, ref, csend_sem.at[0], crecv_sem.at[idx, src], sibling)
-
-    def x_copy(hs):
+    def part_arrival(idx, src, m):
+        ref = precv.at[idx, src, pl.ds(m * tall, tall)]
+        return remote(ref, ref, csend_sem.at[0, m], crecv_sem.at[idx, src, m], sibling)
+
+    def x_copy(hs, m):
+        rows = pl.ds(m * tall, tall)
         return remote(
-            xsend.at[hs], xrecv.at[hs], xsend_sem.at[hs], xrecv_sem.at[hs], (d, (1 - xl) * NY + y)
+            xsend.at[hs, rows], xrecv.at[hs, rows], xsend_sem.at[hs, m], xrecv_sem.at[hs, m],
+            (d, (1 - xl) * NY + y),
         )
 
     def reduce_strip(p):
@@ -259,64 +302,53 @@
 
         @pl.when(zs % NY == y)
         def _():
-            for src in range(NY - 1):
-                part_arrival(idx, src).wait_recv()
             keep = zs // NY == xl
 
             def tile(m, carry):
-                rows = pl.ds(pl.multiple_of(m * 128, 128), 128)
+                for src in range(NY - 1):
+                    part_arrival(idx, src, m).wait_recv()
+                rows = pl.ds(pl.multiple_of(m * tall, tall), tall)
                 value = acc[idx, rows, :]
                 for src in range(NY - 1):
                     value = value + precv[idx, src, rows, :].astype(F32)
                 acc[idx, rows, :] = value
                 xsend[jnp.where(keep, 2, hs), rows, :] = value.astype(BF16)
+
+                @pl.when(jnp.logical_not(keep))
+                def _():
+                    x_copy(hs, m).start()
+
                 return carry
 
-            lax.fori_loop(0, tokens // 128, tile, 0)
-
-            @pl.when(jnp.logical_not(keep))
-            def _():
-                x_copy(hs).start()
+            lax.fori_loop(0, 2, tile, 0)
 
     def step(p, carry):
         zs, hs = place(p)
-        way = p % 2
-
-        @pl.when(p >= 1)
-        def _():
-            z_copy(p, p, sibling, bsend.at[p]).wait_recv()
-
-        @pl.when(p == 1)
-        def _():
-            z_copy(p, 4, zup, bsend.at[p]).start()
-            z_copy(p, 5, zdown, bsend2.at[1]).start()
-
-        @pl.when((p >= 2) & (p <= 10))
-        def _():
-            z_copy(p, p + 4, at((z + NZ + 1 - 2 * way) % NZ, h, c), bsend.at[p]).start()
-
-        @pl.when(p == 13)
-        def _():
-            z_copy(p, 15, zdown, bsend.at[p]).start()
-
-        sib_copy(p).start()
-        sib_copy_in(p).wait_recv()
+        for first in groups:
+
+            @pl.when(p == first)
+            def _(first=first):
+                arrive(first)
+
+        for part in range(2):
+            share(p, part, 1 - c).wait_recv()
         to = zs % NY
         slot = jnp.where(to == y, (zs // NY) * 2 + hs, 4)
 
         def tile(m, inner):
-            rows = pl.ds(pl.multiple_of(m * 256, 256), 256)
+            rows = pl.ds(pl.multiple_of(m * tall, tall), tall)
             right = jnp.concatenate([weights[zs, hs, 0], weights[zs, hs, 1]], axis=1)
             value = jnp.dot(hid[rows, :], right, preferred_element_type=F32)
             acc[slot, rows, :] = value
             psend[p, rows, :] = value.astype(BF16)
+
+            @pl.when(to != y)
+            def _():
+                part_copy(p, m).start()
+
             return inner
 
-        lax.fori_loop(0, tokens // 256, tile, 0)
-
-        @pl.when(to != y)
-        def _():
-            part_copy(p).start()
+        lax.fori_loop(0, 2, tile, 0)
 
         @pl.when(p >= LAG)
         def _():
@@ -330,20 +362,15 @@
         def _():
             grad_step()
 
-        @pl.when(p == 7)
+        @pl.when(p == 11)
         def _():
             grad_two()
 
-        @pl.when(p == 9)
+        @pl.when(p == 15)
         def _():
             grad_three()
 
         return carry
-
-    def sib_copy_in(p):
-        zs, hs = place(p)
-        ref = weights.at[zs, hs, 1 - c]
-        return remote(ref, ref, ssend.at[p], srecv.at[p], sibling)
 
     lax.fori_loop(0, 16, step, 0)
 
@@ -352,46 +379,49 @@
         return carry
 
     lax.fori_loop(16 - LAG, 16, late, 0)
+
+    def last(i, carry):
+        n, m = i // 2, i % 2
+        x_copy(n, m).wait_recv()
+        rows = pl.ds(pl.multiple_of(m * tall, tall), tall)
+        value = acc[xl * 2 + n, rows, :] + xrecv[n, rows, :].astype(F32) + adapt[n, rows, :]
+        out_ref[rows, pl.ds(pl.multiple_of(n * 256, 256), 256)] = value.astype(BF16)
+        return carry
+
+    lax.fori_loop(0, 4, last, 0)
     grad_last()
-    for n in range(2):
-        x_copy(n).wait_recv()
-
-        def last(m, carry, n=n):
-            rows = pl.ds(pl.multiple_of(m * 128, 128), 128)
-            value = acc[xl * 2 + n, rows, :] + xrecv[n, rows, :].astype(F32) + adapt[n, rows, :]
-            out_ref[rows, n * 256 : (n + 1) * 256] = value.astype(BF16)
-            return carry
-
-        lax.fori_loop(0, tokens // 128, last, 0)
-
-    z_copy(0, 2, zup, bsend.at[0]).wait_send()
-    z_copy(0, 3, zdown, bsend2.at[0]).wait_send()
-    seed_copy().wait_send()
-    z_copy(1, 5, zdown, bsend2.at[1]).wait_send()
+
+    for q in range(1, 16):
+        for part in range(2):
+            forward(q, part).wait_send()
 
     def drain(p, carry):
-        @pl.when(((p >= 1) & (p <= 10)) | (p == 13))
-        def _():
-            z_copy(p, p, zup, bsend.at[p]).wait_send()
-
-        sib_copy(p).wait_send()
         zs, hs = place(p)
+        for part in range(2):
+            share(p, part, c).wait_send()
 
         @pl.when(zs % NY != y)
         def _():
-            part_copy(p).wait_send()
+            for m in range(2):
+                part_copy(p, m).wait_send()
 
         return carry
 
     lax.fori_loop(0, 16, drain, 0)
     for n in range(2):
-        x_copy(n).wait_send()
+        for m in range(2):
+            x_copy(n, m).wait_send()
     for j in range(1, NT):
         rank_copy(j).wait_send()
         td_copy(j).wait_send()
         g3_copy(j).wait_send()
     g1_copy().wait_send()
     g2_copy().wait_send()
+
+
+def place_results(*refs):
+    for i in range(3):
+        refs[i + 3][...] = refs[i][...]
 
 
 def shards(hidden, base_weight, adapter_in, adapter_out, cotangent):
@@ -402,13 +432,14 @@
     dma = pltpu.SemaphoreType.DMA
     hbm = pl.BlockSpec(memory_space=pl.ANY)
     vmem = pl.BlockSpec(memory_space=pltpu.VMEM)
-    output, grad_in, grad_out = pl.pallas_call(
+    results = (
+        jax.ShapeDtypeStruct((tokens, cols), BF16),
+        jax.ShapeDtypeStruct((8, ff), F32),
+        jax.ShapeDtypeStruct((8, cols), F32),
+    )
+    made = pl.pallas_call(
         functools.partial(kernel, features),
-        out_shape=(
-            jax.ShapeDtypeStruct((tokens, cols), BF16),
-            jax.ShapeDtypeStruct((8, ff), F32),
-            jax.ShapeDtypeStruct((8, cols), F32),
-        ),
+        out_shape=results,
         in_specs=[hbm] * 5,
         out_specs=(vmem,) * 3,
         scratch_shapes=[
@@ -433,15 +464,14 @@
             pltpu.VMEM((NZ - 1, 16, width // 2), BF16),
             pltpu.VMEM((2, tokens, 256), F32),
             dma((5,)),
-            dma((16,)),
-            dma((3,)),
-            dma((16,)),
-            dma((16,)),
-            dma((16,)),
-            dma((16,)),
-            dma((4, 3)),
-            dma((2,)),
-            dma((2,)),
+            dma((16, 2)),
+            dma((16, 2)),
+            dma((16, 2)),
+            dma((16, 2)),
+            dma((16, 2)),
+            dma((4, 3, 2)),
+            dma((2, 2)),
+            dma((2, 2)),
             dma((7,)),
             dma((7,)),
             dma((7,)),
@@ -456,7 +486,13 @@
         ),
         name="adapter_step",
     )(hidden, base_weight, adapter_in, adapter_out, cotangent)
-    return (output, grad_in, grad_out)
+    return pl.pallas_call(
+        place_results,
+        out_shape=results,
+        in_specs=[vmem] * 3,
+        out_specs=(vmem,) * 3,
+        name="place_results",
+    )(*made)
 
 
 def solution(mesh):

time: 144 us -> 118 us (0.82)
  Pallas kernels: 138 us -> 117 us
  local copies, waits for them, and re-layouts: 4.64 us -> 0 us
    pallas_call x1 -> x2, Pallas kernels: 138 us -> 117 us  [the longest x1 115 us: shards(): pl.pallas_call(functools.partial(kernel, features), out_shape=results, in...]
    unnamed x3 -> x0, local copies, waits for them, and re-layouts: 4.64 us -> none
where the time goes in v2:
time: 118 us
  Pallas kernels  117 us (99%)
    pallas_call x1, Pallas kernels, shards(): pl.pallas_call(functools.partial(kernel, features), out_shape=results, in...  115 us

profile of v2, /device:TPU:6, one launch (start us, length us, event | category | flops | bytes accessed | tf_op | source)
XLA Modules:
  0.0 117.6 jit_solution(9485829846878222481)
XLA Ops:
  0.6 115.1 %adapter_step.1 = (bf16[512,512]{1,0:T(8,128)(2,1)}, f32[8,1792]{1,0:T(8,128)}, f32[8,512]{1,0:T(8,128)}) custom-call(bf16[512,1792]{1,0:T(8,128)(2,1)} %hid_hbm.1, bf16[1792,128]{1,0:T(8,128)(2,1)} %b_hbm.1, bf16[256,1792]{1,0:T(8,128)(2,1)} %ain_hbm.1, bf16[256,512]{1,0:T(8,128)(2,1)} %aout_hbm.1, bf16[512,512]{1,0:T(8,128)(2,1)} %cot_hbm.1), custom_call_target="tpu_custom_call" | custom-call | tf_op jit(solution)/shard_map/adapter_step/pallas_call | solution.py:440
  115.7 1.9 %place_results.1 = (bf16[512,512]{1,0:T(8,128)(2,1)}, f32[8,1792]{1,0:T(8,128)}, f32[8,512]{1,0:T(8,128)}) custom-call(bf16[512,512]{1,0:T(8,128)(2,1)} %get-tuple-element.6.refs_0_, f32[8,1792]{1,0:T(8,128)} %get-tuple-element.7.refs_1_, f32[8,512]{1,0:T(8,128)} %get-tuple-element.8.refs_2_), custom_call_target="tpu_custom_call" | custom-call | tf_op jit(solution)/shard_map/place_results/pallas_call | solution.py:489

commit v3 on v2

--- a/solution.py
+++ b/solution.py
@@ -15,11 +15,10 @@
 NZ, NY, NT = 8, 4, 8
 F32, BF16 = jnp.float32, jnp.bfloat16
 LAST = (((1,), (1,)), ((), ()))
-FIRST = (((0,), (0,)), ((), ()))
-LAG = 8
-OFFSET = (0, 7, 1, 0, 6, 2, 7, 1, 5, 3, 6, 2, 4, 5, 3, 4)
-OTHER = (0, 0, 0, 1, 0, 0, 1, 1, 0, 0, 1, 1, 0, 1, 1, 1)
-SOURCE = (None, 0, 0, 0, 1, 2, 3, 3, 4, 5, 4, 5, None, 10, 11, 12)
+REDUCED = (0, 0, 0, 0, 0, 0, 0, 2, 2, 4, 4, 6, 6, 6, 6, 8)
+OFFSET = (0, 7, 1, 0, 6, 2, 5, 3, 7, 1, 6, 2, 4, 5, 3, 4)
+OTHER = (0, 0, 0, 1, 0, 0, 0, 0, 1, 1, 1, 1, 0, 1, 1, 1)
+SOURCE = (None, 0, 0, 0, 1, 2, 4, 5, 3, 3, 4, 5, None, 10, 11, 12)
 UP, DOWN = (1, 4, 6, 8, 13), (2, 5, 7, 9, 14)
 
 
@@ -37,7 +36,7 @@
     hid_hbm, b_hbm, ain_hbm, aout_hbm, cot_hbm,
     out_ref, gin_ref, gout_ref,
     hid, ain, aout, cot, weights, psend, precv, acc, xsend, xrecv,
-    rsend, rrecv, td, gpart, g1recv, g2send, g2recv, g3send, g3recv, adapt,
+    rsend, rrecv, rcross, td, turned, gpart, g1recv, g2send, g2recv, g3send, g3recv, adapt,
     local_sem, bsend, brecv, ssend, srecv, csend_sem, crecv_sem,
     xsend_sem, xrecv_sem, rsend_sem, rrecv_sem, asend_sem, arecv_sem,
     g12send_sem, g12recv_sem, g3send_sem, g3recv_sem,
@@ -118,20 +117,20 @@
         share(0, part, c).start()
 
     groups = {
-        1: [[(1, (4,)), (2, (5,))]] * 2,
-        3: [[(3, ())]] * 2,
-        4: [[(4, (6, 10)), (5, (7, 11))]] * 2,
-        6: [[(6, (8,)), (7, (9,))]] * 2,
-        8: [[(8, ()), (9, (12,))]] * 2,
-        10: [[(10, ()), (11, ())]] * 2,
-        12: [[(12, (13, 14, 15))]] * 2,
-        13: [[(13, ()), (14, ())]] * 2,
-        15: [[(15, ())]] * 2,
+        1: ((1, (4,)), (2, (5,))),
+        3: ((3, ()),),
+        4: ((4, (6, 10, 8)), (5, (7, 11, 9))),
+        6: ((6, ()), (7, (12,))),
+        8: ((8, ()), (9, ())),
+        10: ((10, (13,)), (11, (14,))),
+        12: ((12, (15,)),),
+        13: ((13, ()), (14, ())),
+        15: ((15, ()),),
     }
 
     def arrive(first):
         for part in range(2):
-            for q, onward in groups[first][part]:
+            for q, onward in groups[first]:
                 arrival(q, part).wait_recv()
                 for n in onward:
                     forward(n, part).start()
@@ -152,41 +151,61 @@
         square = jnp.sum(wide * wide, axis=1, keepdims=True)
         later = lax.dot_general(cot[rows, :], aout[...], LAST, preferred_element_type=F32)
         for jj in range(256 // blk):
-            j = m * (256 // blk) + jj
+            block = m * (256 // blk) + jj
+            j = (block % NY, block // NY)
             cut = slice(jj * blk, (jj + 1) * blk)
-            rsend[j, 0:blk, 0:256] = raw[cut]
-            rsend[j, 0:blk, 256:512] = later[cut]
-            rsend[j, blk : blk + 8, :] = jnp.zeros((8, 512), F32)
-            rsend[j, blk : blk + 1, 0:blk] = jnp.sum(
+            rsend[*j, 0:blk, 0:256] = raw[cut]
+            rsend[*j, 0:blk, 256:512] = later[cut]
+            rsend[*j, blk : blk + 8, :] = jnp.zeros((8, 512), F32)
+            rsend[*j, blk : blk + 1, 0:blk] = jnp.sum(
                 jnp.where(eye, square[cut], 0.0), axis=0, keepdims=True
             )
         return carry
 
     lax.fori_loop(0, tokens // 256, rank_part, 0)
 
-    def rank_copy(j):
-        to = (t + j) % NT
+    flip = (d, (1 - xl) * NY + y)
+
+    def along(i):
+        return (d, xl * NY + (y + i) % NY)
+
+    def rank_copy(i):
         return remote(
-            rsend.at[to], rrecv.at[j - 1], rsend_sem.at[j - 1], rrecv_sem.at[j - 1], (d, to)
+            rsend.at[(y + i) % NY], rrecv.at[i - 1], rsend_sem.at[i - 1], rrecv_sem.at[i - 1], along(i)
         )
 
-    def td_copy(j):
-        to = (t + j) % NT
-        return remote(td.at[t], td.at[t], asend_sem.at[j - 1], arecv_sem.at[j - 1], (d, to))
-
-    def td_arrival(j):
-        ref = td.at[(t + NT - j) % NT]
-        return remote(ref, ref, asend_sem.at[j - 1], arecv_sem.at[j - 1], (d, (t + j) % NT))
-
-    for j in range(1, NT):
-        rank_copy(j).start()
+    def rank_cross():
+        return remote(rsend.at[y, 1 - xl], rcross, rsend_sem.at[3], rrecv_sem.at[3], flip)
+
+    def td_cross():
+        return remote(td.at[t], td.at[t], asend_sem.at[6], arecv_sem.at[6], flip)
+
+    def td_copy(i, side):
+        ref = td.at[(xl + side) % 2 * NY + y]
+        k = side * 3 + i - 1
+        return remote(ref, ref, asend_sem.at[k], arecv_sem.at[k], along(i))
+
+    def td_arrival(i, side):
+        ref = td.at[(xl + side) % 2 * NY + (y + NY - i) % NY]
+        k = side * 3 + i - 1
+        return remote(ref, ref, asend_sem.at[k], arecv_sem.at[k], along(i))
+
+    for i in range(1, NY):
+        rank_copy(i).start()
+
+    def rank_step():
+        for i in range(1, NY):
+            rank_copy(i).wait_recv()
+        for side in range(2):
+            total = rsend[y, side]
+            for i in range(1, NY):
+                total = total + rrecv[i - 1, side]
+            rsend[y, side] = total
+        rank_cross().start()
 
     def tangent_step():
-        for j in range(1, NT):
-            rank_copy(j).wait_recv()
-        total = rsend[t]
-        for j in range(1, NT):
-            total = total + rrecv[j - 1]
+        rank_cross().wait_recv()
+        total = rsend[y, xl] + rcross[...]
         square_sum = jnp.sum(
             jnp.where(eye, total[blk : blk + 1, 0:blk], 0.0), axis=1, keepdims=True
         )
@@ -202,8 +221,15 @@
         dlorentz = phi * later + (coefficient * inner) * lorentz
         td[t, 0] = (phi * lorentz).astype(BF16)
         td[t, 1] = (lift * dlorentz).astype(BF16)
-        for j in range(1, NT):
-            td_copy(j).start()
+        td_cross().start()
+        for i in range(1, NY):
+            td_copy(i, 0).start()
+
+    def tangent_pass():
+        ref = td.at[(1 - xl) * NY + y]
+        remote(ref, ref, asend_sem.at[6], arecv_sem.at[6], flip).wait_recv()
+        for i in range(1, NY):
+            td_copy(i, 1).start()
 
     width = gpart.shape[-1]
     half = width // 2
@@ -222,10 +248,12 @@
         )
 
     def grad_step():
-        for j in range(1, NT):
-            td_arrival(j).wait_recv()
+        for side in range(2):
+            for i in range(1, NY):
+                td_arrival(i, side).wait_recv()
         tangent = td[:, 0].reshape(tokens, 256)
-        draw = td[:, 1].reshape(tokens, 256)
+        turned[0] = tangent.T
+        turned[1] = td[:, 1].reshape(tokens, 256).T
 
         def put(value, cols):
             for k in range(32):
@@ -233,13 +261,13 @@
 
         def in_tile(n, carry):
             cols = pl.ds(pl.multiple_of(n * 256, 256), 256)
-            put(lax.dot_general(draw, hid[:, cols], FIRST, preferred_element_type=F32), cols)
+            put(jnp.dot(turned[1], hid[:, cols], preferred_element_type=F32), cols)
             return carry
 
         lax.fori_loop(0, hid.shape[1] // 256, in_tile, 0)
         for n in range(2):
             cols = slice(n * 256, (n + 1) * 256)
-            part = lax.dot_general(tangent, cot[:, cols], FIRST, preferred_element_type=F32)
+            part = jnp.dot(turned[0], cot[:, cols], preferred_element_type=F32)
             put(adapter_scale * part, slice(hid.shape[1] + n * 256, hid.shape[1] + (n + 1) * 256))
         g1_copy().start()
         for n in range(2):
@@ -322,6 +350,19 @@
 
             lax.fori_loop(0, 2, tile, 0)
 
+    def late(p, carry):
+        reduce_strip(p)
+        return carry
+
+    phases = (
+        (3, rank_step),
+        (5, tangent_step),
+        (5, tangent_pass),
+        (12, grad_step),
+        (14, grad_two),
+        (15, grad_three),
+    )
+
     def step(p, carry):
         zs, hs = place(p)
         for first in groups:
@@ -350,35 +391,19 @@
 
         lax.fori_loop(0, 2, tile, 0)
 
-        @pl.when(p >= LAG)
-        def _():
-            reduce_strip(p - LAG)
-
-        @pl.when(p == 3)
-        def _():
-            tangent_step()
-
-        @pl.when(p == 5)
-        def _():
-            grad_step()
-
-        @pl.when(p == 11)
-        def _():
-            grad_two()
-
-        @pl.when(p == 15)
-        def _():
-            grad_three()
+        lax.fori_loop(look(p - 1, REDUCED), look(p, REDUCED), late, 0)
+
+        for when, phase in phases:
+
+            @pl.when(p == when)
+            def _(phase=phase):
+                phase()
 
         return carry
 
     lax.fori_loop(0, 16, step, 0)
 
-    def late(p, carry):
-        reduce_strip(p)
-        return carry
-
-    lax.fori_loop(16 - LAG, 16, late, 0)
+    lax.fori_loop(REDUCED[-1], 16, late, 0)
 
     def last(i, carry):
         n, m = i // 2, i % 2
@@ -411,10 +436,14 @@
     for n in range(2):
         for m in range(2):
             x_copy(n, m).wait_send()
-    for j in range(1, NT):
-        rank_copy(j).wait_send()
-        td_copy(j).wait_send()
-        g3_copy(j).wait_send()
+    for i in range(1, NY):
+        rank_copy(i).wait_send()
+        td_copy(i, 0).wait_send()
+        td_copy(i, 1).wait_send()
+    rank_cross().wait_send()
+    td_cross().wait_send()
+    for i in range(1, NZ):
+        g3_copy(i).wait_send()
     g1_copy().wait_send()
     g2_copy().wait_send()
 
@@ -453,9 +482,11 @@
             pltpu.VMEM((5, tokens, 256), F32),
             pltpu.VMEM((3, tokens, 256), BF16),
             pltpu.VMEM((2, tokens, 256), BF16),
-            pltpu.VMEM((NT, tokens // NT + 8, 512), F32),
-            pltpu.VMEM((NT - 1, tokens // NT + 8, 512), F32),
+            pltpu.VMEM((NY, 2, tokens // NT + 8, 512), F32),
+            pltpu.VMEM((NY - 1, 2, tokens // NT + 8, 512), F32),
+            pltpu.VMEM((tokens // NT + 8, 512), F32),
             pltpu.VMEM((NT, 2, tokens // NT, rank), BF16),
+            pltpu.VMEM((2, rank, tokens), BF16),
             pltpu.VMEM((2, 2, NZ, 8, width), F32),
             pltpu.VMEM((2, NZ, 8, width), F32),
             pltpu.VMEM((NZ * 8, width), BF16),
@@ -472,8 +503,8 @@
             dma((4, 3, 2)),
             dma((2, 2)),
             dma((2, 2)),
-            dma((7,)),
-            dma((7,)),
+            dma((4,)),
+            dma((4,)),
             dma((7,)),
             dma((7,)),
             dma((2,)),

time: 118 us -> 104 us (0.88); the launches traced: 118 us -> 102 us
  Pallas kernels: 117 us -> 101 us
    pallas_call x1, Pallas kernels: 115 us -> 99.2 us  [shards(): pl.pallas_call(functools.partial(kernel, features), out_shape=results, in...]
where the time goes in v3:
time: 104 us; the launch traced here: 102 us
  Pallas kernels  101 us (97%)
    pallas_call x1, Pallas kernels, shards(): pl.pallas_call(functools.partial(kernel, features), out_shape=results, in...  99.2 us

profile of v3, /device:TPU:6, one launch (start us, length us, event | category | flops | bytes accessed | tf_op | source)
XLA Modules:
  0.0 101.7 jit_solution(18243700146311029080)
XLA Ops:
  0.6 99.2 %adapter_step.1 = (bf16[512,512]{1,0:T(8,128)(2,1)}, f32[8,1792]{1,0:T(8,128)}, f32[8,512]{1,0:T(8,128)}) custom-call(bf16[512,1792]{1,0:T(8,128)(2,1)} %hid_hbm.1, bf16[1792,128]{1,0:T(8,128)(2,1)} %b_hbm.1, bf16[256,1792]{1,0:T(8,128)(2,1)} %ain_hbm.1, bf16[256,512]{1,0:T(8,128)(2,1)} %aout_hbm.1, bf16[512,512]{1,0:T(8,128)(2,1)} %cot_hbm.1), custom_call_target="tpu_custom_call" | custom-call | tf_op jit(solution)/shard_map/adapter_step/pallas_call | solution.py:469
  99.8 1.9 %place_results.1 = (bf16[512,512]{1,0:T(8,128)(2,1)}, f32[8,1792]{1,0:T(8,128)}, f32[8,512]{1,0:T(8,128)}) custom-call(bf16[512,512]{1,0:T(8,128)(2,1)} %get-tuple-element.6.refs_0_, f32[8,1792]{1,0:T(8,128)} %get-tuple-element.7.refs_1_, f32[8,512]{1,0:T(8,128)} %get-tuple-element.8.refs_2_), custom_call_target="tpu_custom_call" | custom-call | tf_op jit(solution)/shard_map/place_results/pallas_call | solution.py:520

commit v4 on v3

--- a/solution.py
+++ b/solution.py
@@ -117,20 +117,20 @@
         share(0, part, c).start()
 
     groups = {
-        1: ((1, (4,)), (2, (5,))),
-        3: ((3, ()),),
-        4: ((4, (6, 10, 8)), (5, (7, 11, 9))),
-        6: ((6, ()), (7, (12,))),
-        8: ((8, ()), (9, ())),
-        10: ((10, (13,)), (11, (14,))),
-        12: ((12, (15,)),),
-        13: ((13, ()), (14, ())),
-        15: ((15, ()),),
+        1: [((1, (4,)), (2, (5,)))] * 2,
+        3: [((3, ()),)] * 2,
+        4: [((4, (6, 10)), (5, (7, 11))), ((4, (6, 10)), (5, (7, 11)))],
+        6: [((6, (8,)), (7, (9, 12))), ((6, (8,)), (7, (9, 12)))],
+        8: [((8, ()), (9, ()))] * 2,
+        10: [((10, (13,)), (11, (14,)))] * 2,
+        12: [((12, (15,)),)] * 2,
+        13: [((13, ()), (14, ()))] * 2,
+        15: [((15, ()),)] * 2,
     }
 
     def arrive(first):
         for part in range(2):
-            for q, onward in groups[first]:
+            for q, onward in groups[first][part]:
                 arrival(q, part).wait_recv()
                 for n in onward:
                     forward(n, part).start()
@@ -354,13 +354,8 @@
         reduce_strip(p)
         return carry
 
-    phases = (
-        (3, rank_step),
-        (5, tangent_step),
-        (5, tangent_pass),
-        (12, grad_step),
-        (14, grad_two),
-        (15, grad_three),
+    phases = ((3, rank_step), (5, tangent_step), (7, tangent_pass)) + (
+        (12, grad_step), (14, grad_two), (15, grad_three),
     )
 
     def step(p, carry):

time: 104 us -> 100 us (0.962); the launches traced: 102 us -> 99.7 us
  Pallas kernels: 101 us -> 99.1 us
    pallas_call x1, Pallas kernels: 99.2 us -> 97.2 us  [shards(): pl.pallas_call(functools.partial(kernel, features), out_shape=results, in...]
where the time goes in v4:
time: 100 us; the launch traced here: 99.7 us
  Pallas kernels  99.1 us (99%)
    pallas_call x1, Pallas kernels, shards(): pl.pallas_call(functools.partial(kernel, features), out_shape=results, in...  97.2 us

profile of v4, /device:TPU:6, one launch (start us, length us, event | category | flops | bytes accessed | tf_op | source)
XLA Modules:
  0.0 99.7 jit_solution(2235038100800357114)
XLA Ops:
  0.6 97.2 %adapter_step.1 = (bf16[512,512]{1,0:T(8,128)(2,1)}, f32[8,1792]{1,0:T(8,128)}, f32[8,512]{1,0:T(8,128)}) custom-call(bf16[512,1792]{1,0:T(8,128)(2,1)} %hid_hbm.1, bf16[1792,128]{1,0:T(8,128)(2,1)} %b_hbm.1, bf16[256,1792]{1,0:T(8,128)(2,1)} %ain_hbm.1, bf16[256,512]{1,0:T(8,128)(2,1)} %aout_hbm.1, bf16[512,512]{1,0:T(8,128)(2,1)} %cot_hbm.1), custom_call_target="tpu_custom_call" | custom-call | tf_op jit(solution)/shard_map/adapter_step/pallas_call | solution.py:464
  97.8 1.9 %place_results.1 = (bf16[512,512]{1,0:T(8,128)(2,1)}, f32[8,1792]{1,0:T(8,128)}, f32[8,512]{1,0:T(8,128)}) custom-call(bf16[512,512]{1,0:T(8,128)(2,1)} %get-tuple-element.6.refs_0_, f32[8,1792]{1,0:T(8,128)} %get-tuple-element.7.refs_1_, f32[8,512]{1,0:T(8,128)} %get-tuple-element.8.refs_2_), custom_call_target="tpu_custom_call" | custom-call | tf_op jit(solution)/shard_map/place_results/pallas_call | solution.py:515

commit v5 on v4

--- a/solution.py
+++ b/solution.py
@@ -371,20 +371,17 @@
         to = zs % NY
         slot = jnp.where(to == y, (zs // NY) * 2 + hs, 4)
 
-        def tile(m, inner):
-            rows = pl.ds(pl.multiple_of(m * tall, tall), tall)
-            right = jnp.concatenate([weights[zs, hs, 0], weights[zs, hs, 1]], axis=1)
-            value = jnp.dot(hid[rows, :], right, preferred_element_type=F32)
-            acc[slot, rows, :] = value
-            psend[p, rows, :] = value.astype(BF16)
-
-            @pl.when(to != y)
-            def _():
+        right = jnp.concatenate([weights[zs, hs, 0], weights[zs, hs, 1]], axis=1)
+        value = jnp.dot(hid[...], right, preferred_element_type=F32)
+        for m in range(2):
+            cut = slice(m * tall, (m + 1) * tall)
+            psend[p, cut, :] = value[cut].astype(BF16)
+            acc[slot, cut, :] = value[cut]
+
+        @pl.when(to != y)
+        def _():
+            for m in range(2):
                 part_copy(p, m).start()
-
-            return inner
-
-        lax.fori_loop(0, 2, tile, 0)
 
         lax.fori_loop(look(p - 1, REDUCED), look(p, REDUCED), late, 0)
 

time: 100 us -> 100 us (level)
  no operation moved by 1% of the time
where the time goes in v5:
time: 100 us
  Pallas kernels  99.5 us (100%)
    pallas_call x1, Pallas kernels, shards(): pl.pallas_call(functools.partial(kernel, features), out_shape=results, in...  97.6 us

profile of v5, /device:TPU:6, one launch (start us, length us, event | category | flops | bytes accessed | tf_op | source)
XLA Modules:
  0.0 100.1 jit_solution(17995075005475373635)
XLA Ops:
  0.6 97.6 %adapter_step.1 = (bf16[512,512]{1,0:T(8,128)(2,1)}, f32[8,1792]{1,0:T(8,128)}, f32[8,512]{1,0:T(8,128)}) custom-call(bf16[512,1792]{1,0:T(8,128)(2,1)} %hid_hbm.1, bf16[1792,128]{1,0:T(8,128)(2,1)} %b_hbm.1, bf16[256,1792]{1,0:T(8,128)(2,1)} %ain_hbm.1, bf16[256,512]{1,0:T(8,128)(2,1)} %aout_hbm.1, bf16[512,512]{1,0:T(8,128)(2,1)} %cot_hbm.1), custom_call_target="tpu_custom_call" | custom-call | tf_op jit(solution)/shard_map/adapter_step/pallas_call | solution.py:461
  98.2 1.9 %place_results.1 = (bf16[512,512]{1,0:T(8,128)(2,1)}, f32[8,1792]{1,0:T(8,128)}, f32[8,512]{1,0:T(8,128)}) custom-call(bf16[512,512]{1,0:T(8,128)(2,1)} %get-tuple-element.6.refs_0_, f32[8,1792]{1,0:T(8,128)} %get-tuple-element.7.refs_1_, f32[8,512]{1,0:T(8,128)} %get-tuple-element.8.refs_2_), custom_call_target="tpu_custom_call" | custom-call | tf_op jit(solution)/shard_map/place_results/pallas_call | solution.py:512
